TPU v7x, 512 devices: a whole 4x4x16 slice. The times are simulated.
512 devices in a mesh: term: 16 (over z), doc: 32 (over x, y, core).
Axes of the slice: x: 4, y: 4, z: 16, core: 2. Of those that a mesh axis runs over, the one named last changes fastest.
Arguments:
- postings: bfloat16 [16384, 30720], P('doc', 'term'), may hold values from 0 to 3
- query_terms: int32 [128, 32], replicated, may hold values from 0 to 30719
- query_levels: int32 [128, 32], replicated, may hold values from 1 to 255
- feedback_ids: int32 [128, 10], replicated, may hold values from 0 to 16383, as said below
Outputs:
- first_scores: float32 [128, 16384], P('term', 'doc')
- final_scores: float32 [128, 16384], P('term', 'doc')
Inputs may be any that keep to these rules, and one draw needn't show every extreme that they name: `feedback_ids`: the 1280 feedback ids are all different.
All inputs are finite; a program needn't handle non-finite values.
Results may differ from a plain program's by a relative error of at most 0.0015.
Values may be sent and summed in bfloat16 or wider, within the bound.
No kernel may reach another device: no remote copies, remote signals or barrier semaphores. Data moves between devices by JAX's collectives and lax.ppermute only.
A program may use at most 64 MiB of HBM per device.

v0:
```python
import jax
import jax.numpy as jnp
from jax import lax
from jax.sharding import PartitionSpec as P

expansion_weight = 0.25


def query_slice(query_terms, query_levels, width, offset):
    columns = offset + lax.iota(jnp.int32, width)

    def add_term(position, total):
        ids_now = lax.dynamic_index_in_dim(query_terms, position, 1, keepdims=True)
        weight_now = (
            lax.dynamic_index_in_dim(query_levels, position, 1, keepdims=True).astype(jnp.float32)
            / 100.0
        )
        return total + jnp.where(ids_now == columns[None, :], weight_now, 0.0)

    initial = jnp.zeros((query_terms.shape[0], width), jnp.float32)
    return lax.fori_loop(0, query_terms.shape[1], add_term, initial)


def score_block(query_rows, postings):
    return lax.dot_general(
        query_rows, postings, (((1,), (1,)), ((), ())), preferred_element_type=jnp.float32
    )


def per_device(postings, query_terms, query_levels, feedback_ids):
    doc_rows, width = postings.shape
    queries = query_terms.shape[0]
    term_groups = lax.axis_size("term")
    group_rows = queries // term_groups
    term_index = lax.axis_index("term")
    doc_index = lax.axis_index("doc")
    query_part = query_slice(query_terms, query_levels, width, term_index * width)
    query_rounded = query_part.astype(jnp.bfloat16)
    local_slot = feedback_ids - doc_index * doc_rows
    positions = lax.iota(jnp.int32, doc_rows)
    selector = (local_slot[:, :, None] == positions[None, None, :]).astype(jnp.float32)
    partial_scores = score_block(query_rounded, postings)
    first_all = lax.psum(partial_scores, "term")
    first_scores = lax.dynamic_slice_in_dim(first_all, term_index * group_rows, group_rows, 0)
    feedback = jnp.sum(selector * first_all[:, None, :], axis=2).astype(jnp.bfloat16)
    feedback_wide = feedback.astype(jnp.float32)
    mixing = jnp.sum(selector * feedback_wide[:, :, None], axis=1).astype(jnp.bfloat16)
    numerator = jnp.dot(mixing, postings, preferred_element_type=jnp.float32)
    weight_part = jnp.sum(feedback_wide, axis=1)
    numerator_all, weight_sum = lax.psum((numerator, weight_part), "doc")
    expanded = (query_part + expansion_weight * numerator_all / weight_sum[:, None]).astype(
        jnp.bfloat16
    )
    final_scores = lax.psum_scatter(
        score_block(expanded, postings), "term", scatter_dimension=0, tiled=True
    )
    return (first_scores, final_scores)


def solution(mesh):
    return jax.shard_map(
        per_device,
        mesh=mesh,
        in_specs=(P("doc", "term"), P(), P(), P()),
        out_specs=(P("term", "doc"), P("term", "doc")),
        check_vma=False,
    )
```

profile of v0, /device:TPU:6, one launch (start us, length us, event | category | flops | bytes accessed | tf_op | source)
XLA Modules:
  0.0 416.9 jit_solution(17886859265091422871)
XLA Ops:
  7.2 53.6 %while.14 = (s32[]{:T(128)}, f32[128,1920]{1,0:T(8,128)S(1)}, s32[128,32]{0,1:T(8,128)}, s32[128,32]{0,1:T(8,128)}, s32[]{:T(128)}, /*index=5*/s32[]{:T(128)}, s32[]{:T(128)}) while((s32[]{:T(128)}, f32[128,1920]{1,0:T(8,128)S(1)}, s32[128,32]{0,1:T(8,128)}, s32[128,32]{0,1:T(8,128)}, s32[]{:T(128)}, /*index=5*/s32[]{:T(128)}, ...), condition=%wide.region_1.2_spmd.clone, body=%wide.region_0.1_spmd.clone.sunk | while | flops 985219 | bytes 1984619 | solution.py:21
  7.3 0.8 multiply_bitcast_fusion.2
  9.1 0.7 multiply_bitcast_fusion.2
  10.7 0.7 multiply_bitcast_fusion.2
  14.1 0.7 multiply_bitcast_fusion.2
  15.7 0.7 multiply_bitcast_fusion.2
  17.4 0.7 multiply_bitcast_fusion.2
  19.1 0.7 multiply_bitcast_fusion.2
  22.4 0.7 multiply_bitcast_fusion.2
  24.1 0.7 multiply_bitcast_fusion.2
  27.4 0.7 multiply_bitcast_fusion.2
  29.1 0.7 multiply_bitcast_fusion.2
  32.4 0.7 multiply_bitcast_fusion.2
  34.1 0.7 multiply_bitcast_fusion.2
  35.8 0.7 multiply_bitcast_fusion.2
  37.5 0.7 multiply_bitcast_fusion.2
  40.8 0.7 multiply_bitcast_fusion.2
  42.5 0.7 multiply_bitcast_fusion.2
  45.8 0.7 multiply_bitcast_fusion.2
  47.5 0.7 multiply_bitcast_fusion.2
  49.2 0.7 multiply_bitcast_fusion.2
  50.8 0.7 multiply_bitcast_fusion.2
  54.2 0.7 multiply_bitcast_fusion.2
  60.9 1.5 fusion.5
  62.4 140.0 %all-reduce.3.cloned.1.call-done = f32[128,512]{1,0:T(8,128)} async-done(((f32[128,512]{1,0:T(8,128)}), f32[128,512]{1,0:T(8,128)}) %all-reduce.3.cloned.1.call-update) | async-done | bytes 262160 | tf_op jit(solution)/shard_map/psum | solution.py:43
  202.4 1.5 select_reduce_fusion.1
  204.4 1.4 fusion.11
  205.9 53.0 %psum.23 = f32[128]{0:T(128)S(1)} all-reduce(f32[128]{0:T(128)S(1)} %fusion.9), channel_id=1, replica_groups=mesh['term'=16,'doc'=32] {'doc'}, use_global_device_ids=true, to_apply=%region_7.8 | all-reduce | flops 128 | bytes 1024 | tf_op jit(solution)/shard_map/psum | solution.py:50
  258.9 79.8 %all-reduce.5.cloned.1.call-done = f32[128,1920]{1,0:T(8,128)} async-done(((f32[128,1920]{1,0:T(8,128)}), f32[128,1920]{1,0:T(8,128)}) %all-reduce.5.cloned.1.call-update) | async-done | bytes 983056 | tf_op jit(solution)/shard_map/psum | solution.py:50
  338.7 2.7 fusion.2
  341.4 1.3 constant_dynamic-slice_fusion
  342.8 67.6 %reduce-scatter.2.cloned.1.call-done = f32[8,512]{1,0:T(8,128)} async-done(((f32[128,512]{1,0:T(8,128)}), f32[8,512]{1,0:T(8,128)}) %reduce-scatter.2.cloned.1.call-update) | async-done | bytes 16400 | tf_op jit(solution)/shard_map/reduce_scatter | solution.py:54
  (121 shorter events, 37.9 us)
Async XLA Ops:
  7.2 53.7 %copy-start = (bf16[512,1920]{1,0:T(8,128)(2,1)S(1)}, bf16[512,1920]{1,0:T(8,128)(2,1)}, u32[]{:S(2)}) copy-start(bf16[512,1920]{1,0:T(8,128)(2,1)} %param.6) | copy-start | bytes 5898244
  7.2 195.3 %all-reduce.3.cloned.1.call-start = ((), (), s32[]{:S(2)}) async-start(), calls=%async_computation.1 | async-start | bytes 524288 | tf_op jit(solution)/shard_map/psum | solution.py:43
  60.8 1.6 copy-start.1
  62.4 276.4 %all-reduce.5.cloned.1.call-start = ((), (), s32[]{:S(2)}) async-start(), calls=%async_computation.2 | async-start | bytes 1966080 | tf_op jit(solution)/shard_map/psum | solution.py:50
  205.8 204.5 %reduce-scatter.2.cloned.1.call-start = ((), (), s32[]{:S(2)}) async-start(), calls=%async_computation.3 | async-start | bytes 278528 | tf_op jit(solution)/shard_map/reduce_scatter | solution.py:54
Sparse Core Ops, SparseCore 0:
  62.5 139.9 all-reduce.2
  206.0 132.6 all-reduce.4
  342.1 68.2 reduce-scatter.1
where the time goes:
time: 420 us; the launch traced here: 417 us
  waiting for transfers between devices  287 us (68%)
  blocking collectives  53 us (13%)
  other arithmetic  32.6 us (8%)
  local copies, waits for them, and re-layouts  23.5 us (6%)
  between operations  13.8 us (3%)
  matrix products  5.59 us (1%)
    psum x1, waiting for transfers between devices, per_device(): first_all = lax.psum(partial_scores, 'term')  140 us
    psum x1, waiting for transfers between devices, per_device(): numerator_all, weight_sum = lax.psum((numerator, weight_part), 'doc')  79.8 us
    reduce_scatter x1, waiting for transfers between devices, per_device(): lax.psum_scatter(score_block(expanded, postings), 'term', scatter_dimensi...  67.6 us
    psum x1, blocking collectives, per_device(): numerator_all, weight_sum = lax.psum((numerator, weight_part), 'doc')  53 us
    broadcast_in_dim x32, other arithmetic, add_term(): return total + jnp.where(ids_now == columns[None, :], weight_now, 0.0)  22.5 us
    eq x32, local copies, waits for them, and re-layouts, add_term(): return total + jnp.where(ids_now == columns[None, :], weight_now, 0.0)  22.1 us
  transfers between devices with their start and end apart: 3, of which 3 were waited for; matrix products, arithmetic and copies ran while one was open for 0% of the time, Pallas kernels for 0%

commit v1 on v0

v1 whole, which is shorter than its diff:
```python
import jax
import jax.numpy as jnp
from jax import lax
from jax.sharding import PartitionSpec as P

expansion_weight = 0.25


def query_slice(query_terms, query_levels, width, offset):
    columns = offset + lax.iota(jnp.int32, width)
    total = jnp.zeros((query_terms.shape[0], width), jnp.int32)
    for k in range(query_terms.shape[1]):
        hit = query_terms[:, k : k + 1] == columns[None, :]
        total = total + jnp.where(hit, query_levels[:, k : k + 1], 0)
    return total.astype(jnp.float32) / 100.0


def score_block(query_rows, postings):
    return lax.dot_general(
        query_rows, postings, (((1,), (1,)), ((), ())), preferred_element_type=jnp.float32
    )


def per_device(postings, query_terms, query_levels, feedback_ids):
    doc_rows, width = postings.shape
    queries = query_terms.shape[0]
    terms = lax.axis_size("term")
    docs = lax.axis_size("doc")
    group = queries // terms
    chunk = queries // docs
    term_index = lax.axis_index("term")
    doc_index = lax.axis_index("doc")
    query_part = query_slice(query_terms, query_levels, width, term_index * width)
    partial = score_block(query_part.astype(jnp.bfloat16), postings)

    positions = doc_index * doc_rows + lax.iota(jnp.int32, doc_rows)
    member = jnp.zeros((queries, doc_rows), jnp.bool_)
    for j in range(feedback_ids.shape[1]):
        member = member | (feedback_ids[:, j : j + 1] == positions[None, :])
    chosen = jnp.sum(jnp.where(member, partial, 0.0), axis=0)

    chosen_all = lax.all_to_all(
        jnp.broadcast_to(chosen.reshape(1, 4, doc_rows // 4), (terms, 4, doc_rows // 4)), "term", 0, 0
    )
    weight = jnp.sum(chosen_all, axis=0).reshape(doc_rows).astype(jnp.bfloat16)
    mixing = jnp.where(member, weight[None, :], jnp.zeros((), jnp.bfloat16))
    numerator = jnp.dot(mixing, postings, preferred_element_type=jnp.float32)
    weight_part = jnp.sum(mixing.astype(jnp.float32), axis=1, keepdims=True)
    high = weight_part.astype(jnp.bfloat16).astype(jnp.float32)
    pair = jnp.concatenate([high, weight_part - high], axis=1)
    pair = jnp.pad(pair, ((0, 0), (0, 126)))
    packed = jnp.concatenate([numerator, pair], axis=1).astype(jnp.bfloat16)
    shares = lax.all_to_all(packed.reshape(docs, chunk, width + 128), "doc", 0, 0)
    total = jnp.sum(shares.astype(jnp.float32), axis=0)
    weight_sum = total[:, width : width + 1] + total[:, width + 1 : width + 2]
    own = lax.dynamic_slice_in_dim(query_part, doc_index * chunk, chunk, 0)
    expanded_own = (own + expansion_weight * total[:, :width] / weight_sum).astype(jnp.bfloat16)
    expanded = lax.all_to_all(
        jnp.broadcast_to(expanded_own[None], (docs, chunk, width)), "doc", 0, 0
    ).reshape(queries, width)
    final = score_block(expanded, postings)
    both = jnp.stack([partial.reshape(terms, group, doc_rows), final.reshape(terms, group, doc_rows)], axis=1)
    both = both.astype(jnp.bfloat16).reshape(terms, 2 * group, doc_rows)
    sums = jnp.sum(lax.all_to_all(both, "term", 0, 0).astype(jnp.float32), axis=0)
    return (sums[:group], sums[group:])


def solution(mesh):
    return jax.shard_map(
        per_device,
        mesh=mesh,
        in_specs=(P("doc", "term"), P(), P(), P()),
        out_specs=(P("term", "doc"), P("term", "doc")),
        check_vma=False,
    )
```

time: 420 us -> 99.9 us (0.24)
  the two profiles are of different devices: /device:TPU:6 before, /device:TPU:33 now
where the time goes in v1:
time: 99.9 us; the launch traced here: 99.4 us
  blocking collectives  61.5 us (62%)
  waiting for transfers between devices  11.6 us (12%)
  starting transfers between devices  9.17 us (9%)
  local copies, waits for them, and re-layouts  7.11 us (7%)
  other arithmetic  5.36 us (5%)
  matrix products  3.83 us (4%)
    all_to_all x1, blocking collectives, per_device(): lax.all_to_all(jnp.broadcast_to(chosen.reshape(1, 4, doc_rows // 4), (ter...  25 us
    all_to_all x1, blocking collectives, per_device(): lax.all_to_all(both, 'term', 0, 0).astype(jnp.float32)  21.8 us
    all_to_all x1, blocking collectives, per_device(): lax.all_to_all(jnp.broadcast_to(expanded_own[None], (docs, chunk, width))...  14.7 us
    all_to_all x1, waiting for transfers between devices, per_device(): lax.all_to_all(packed.reshape(docs, chunk, width + 128), 'doc', 0, 0)  11.6 us
    all_to_all x1, starting transfers between devices, per_device(): lax.all_to_all(packed.reshape(docs, chunk, width + 128), 'doc', 0, 0)  9.17 us
    div x1, other arithmetic, query_slice(): return total.astype(jnp.float32) / 100.0  3.18 us
    dot_general x2, matrix products, score_block(): lax.dot_general(query_rows, postings, (((1,), (1,)), ((), ())), preferred...  2.23 us
  transfers between devices with their start and end apart: 1, of which 1 were waited for; matrix products, arithmetic and copies ran while one was open for 0% of the time, Pallas kernels for 0%

profile of v1, /device:TPU:33, one launch (start us, length us, event | category | flops | bytes accessed | tf_op | source)
XLA Modules:
  0.0 99.4 jit_solution(16453494153829960827)
XLA Ops:
  0.6 0.0 copy-start
  0.6 1.0 slice_bitcast_fusion.71
  1.6 1.0 %slice_bitcast_fusion.73 = (s32[128]{0:T(128)S(1)}, s32[128]{0:T(128)S(1)}, s32[128]{0:T(128)S(1)}, s32[128]{0:T(128)S(1)}, s32[128]{0:T(128)S(1)}, /*index=5*/s...) fusion(s32[128,32]{0,1:T(8,128)} %param.5), kind=kLoop, calls=%fused_computation.105 | loop fusion | bytes 19456 | tf_op jit(solution)/shard_map/eq | solution.py:13
  2.6 1.0 slice_bitcast_fusion.70
  3.6 1.0 %slice_bitcast_fusion.72 = (s32[128]{0:T(128)S(1)}, s32[128]{0:T(128)S(1)}, s32[128]{0:T(128)S(1)}, s32[128]{0:T(128)S(1)}, s32[128]{0:T(128)S(1)}, /*index=5*/s...) fusion(s32[128,32]{0,1:T(8,128)} %param.6), kind=kLoop, calls=%fused_computation.104 | loop fusion | bytes 19456 | tf_op jit(solution)/shard_map/jit(_where)/broadcast_in_dim | solution.py:14
  4.6 1.0 slice_bitcast_fusion.9
  5.6 3.2 %convert_multiply_fusion = f32[128,1920]{1,0:T(8,128)S(1)} fusion(s32[128]{0:T(128)S(1)} %get-tuple-element.68, s32[128]{0:T(128)S(1)} %get-tuple-element.69, s32[128]{0:T(128)S(1)} %get-tuple-element.39, s32[128]{0:T(128)S(1)} %get-tuple-element.40, s32[128]{0:T(128)S(1)} %get-tuple-element.41, s32[128]{0:T(128)S(1)} %get-tuple-element.42, ...), kind=kLoop, calls=%fused_computation.6 | loop fusion | flops 23838720 | bytes 1023488 | tf_op jit(solution)/shard_map/div | solution.py:15
  8.8 0.0 copy-done
  8.8 1.5 %convert_bitcast_fusion = (bf16[16,1,8,512]{3,2,0,1:T(8,128)(2,1)}, f32[512]{0:T(512)S(1)}) fusion(s32[128]{0:T(128)S(1)} %get-tuple-element.78, s32[128]{0:T(128)S(1)} %get-tuple-element.79, s32[128]{0:T(128)S(1)} %get-tuple-element.71, s32[128]{0:T(128)S(1)} %get-tuple-element.72, s32[128]{0:T(128)S(1)} %get-tuple-element.73, ...), kind=kOutput, calls=%fused_computation.17 | convolution fusion | flops 253345280 | bytes 3089408 | tf_op jit(solution)/shard_map/dot_general | solution.py:19
  10.3 25.0 %all_to_all.20 = f32[16,4,128]{2,1,0:T(4,128)S(1)} all-to-all(f32[16,4,128]{2,1,0:T(4,128)S(1)} %broadcast_in_dim.402), channel_id=1, replica_groups=mesh['term'=16,'doc'=32] {'term'}, dimensions={0} | all-to-all | bytes 65536 | tf_op jit(solution)/shard_map/all_to_all | solution.py:42
  35.4 0.5 convert_reduce_fusion.2
  35.8 1.6 %convolution_convert_fusion = bf16[128,1920]{1,0:T(8,128)(2,1)} fusion(bf16[512,1920]{1,0:T(8,128)(2,1)S(1)} %copy-done, bf16[512]{0:T(512)(128)(2,1)S(1)} %bitcast.178, s32[512]{0:T(512)S(1)} %iota_add_fusion.1, s32[128]{0:T(128)S(1)} %get-tuple-element.78, s32[128]{0:T(128)S(1)} %get-tuple-element.79, s32[128]{0:T(128)S(1)} %get-tuple-element.71, ...), kind=kOutput, calls=%fused_computation | convolution fusion | flops 253214720 | bytes 2465792 | tf_op jit(solution)/shard_map/dot_general | solution.py:47
  37.4 0.1 copy.21
  37.6 1.1 %concatenate.13 = bf16[32,4,1920]{2,1,0:T(4,128)(2,1)S(1)} reshape(bf16[128,1920]{1,0:T(8,128)(2,1)} %convolution_convert_fusion) | data formatting | bytes 983040 | tf_op jit(solution)/shard_map/concatenate | solution.py:52
  38.7 1.1 %pad_maximum_fusion = bf16[32,4,2048]{2,1,0:T(4,128)(2,1)} fusion(bf16[32,4,128]{2,1,0:T(4,128)(2,1)S(1)} %bitcast.176, bf16[32,4,1920]{2,1,0:T(4,128)(2,1)S(1)} %concatenate.13), kind=kLoop, calls=%fused_computation.7 | loop fusion | flops 1048576 | bytes 1048576 | tf_op jit(solution)/shard_map/concatenate | solution.py:52
  39.9 9.2 %all-to-all-start.1 = ((bf16[32,4,2048]{2,1,0:T(4,128)(2,1)}), bf16[32,4,2048]{2,1,0:T(4,128)(2,1)S(1)}, u32[]{:S(2)}, u32[]{:S(2)}) async-start(bf16[32,4,2048]{2,1,0:T(4,128)(2,1)} %pad_maximum_fusion), calls=%async_computation.1 | async-start | bytes 1048576 | tf_op jit(solution)/shard_map/all_to_all | solution.py:53
  49.0 11.6 %all-to-all-done.1 = bf16[32,4,2048]{2,1,0:T(4,128)(2,1)S(1)} async-done(((bf16[32,4,2048]{2,1,0:T(4,128)(2,1)}), bf16[32,4,2048]{2,1,0:T(4,128)(2,1)S(1)}, u32[]{:S(2)}, u32[]{:S(2)}) %all-to-all-start.1) | async-done | bytes 524320 | tf_op jit(solution)/shard_map/all_to_all | solution.py:53
  60.7 0.2 convert_reduce_fusion
  60.9 0.2 fusion.14
  61.1 0.1 fusion.13
  61.2 0.1 broadcast_in_dim.405
  61.3 14.7 %all_to_all.21 = bf16[32,4,1920]{2,1,0:T(4,128)(2,1)S(1)} all-to-all(bf16[32,4,1920]{2,1,0:T(4,128)(2,1)S(1)} %broadcast_in_dim.405), channel_id=1, replica_groups=mesh['term'=16,'doc'=32] {'doc'}, dimensions={0} | all-to-all | bytes 983040 | tf_op jit(solution)/shard_map/all_to_all | solution.py:58
  76.0 0.0 copy-start.1
  76.0 0.1 reshape.59
  76.1 0.8 fusion.5
  76.9 0.0 copy-done.1
  77.0 21.8 %all_to_all.22 = bf16[16,16,512]{2,1,0:T(8,128)(2,1)S(1)} all-to-all(bf16[16,16,512]{2,1,0:T(8,128)(2,1)S(1)} %copy_bitcast_fusion), channel_id=1, replica_groups=mesh['term'=16,'doc'=32] {'term'}, dimensions={0} | all-to-all | bytes 524288 | tf_op jit(solution)/shard_map/all_to_all | solution.py:64
  98.8 0.6 fusion.17
  (10 shorter events, 0.1 us)
Async XLA Ops:
  0.6 8.2 %copy-start = (bf16[512,1920]{1,0:T(8,128)(2,1)S(1)}, bf16[512,1920]{1,0:T(8,128)(2,1)}, u32[]{:S(2)}) copy-start(bf16[512,1920]{1,0:T(8,128)(2,1)} %param.4) | copy-start | bytes 5898244
  39.9 20.8 %all-to-all-start.1 = ((bf16[32,4,2048]{2,1,0:T(4,128)(2,1)}), bf16[32,4,2048]{2,1,0:T(4,128)(2,1)S(1)}, u32[]{:S(2)}, u32[]{:S(2)}) async-start(bf16[32,4,2048]{2,1,0:T(4,128)(2,1)} %pad_maximum_fusion), calls=%async_computation.1 | async-start | bytes 1048576 | tf_op jit(solution)/shard_map/all_to_all | solution.py:53
  76.0 0.9 copy-start.1

commit v2 on v0

v2 whole, which is shorter than its diff:
```python
import jax
import jax.numpy as jnp
from jax import lax
from jax.experimental import pallas as pl
from jax.experimental.pallas import tpu as pltpu
from jax.sharding import PartitionSpec as P

expansion_weight = 0.25
lanes = 128
half = 1024
f32 = jnp.float32
bf16 = jnp.bfloat16
VMEM = pl.BlockSpec(memory_space=pltpu.VMEM)


def dot_nt(a, b):
    return lax.dot_general(a, b, (((1,), (1,)), ((), ())), preferred_element_type=f32)


def iota(shape, axis):
    return lax.broadcasted_iota(jnp.int32, shape, axis)


def first_round(terms_ref, levels_ref, ids_ref, postings_hbm, send_ref, mask_ref, query_ref,
                postings_ref, sem):
    copy = pltpu.make_async_copy(postings_hbm, postings_ref, sem)
    copy.start()
    slots, queries = terms_ref.shape
    docs, width = postings_ref.shape
    tiles = width // lanes
    spread = 8 * slots
    local = terms_ref[...] - lax.axis_index("term") * width
    tile_of = lax.shift_right_arithmetic(local, 7)
    lane_of = local & 127
    repeat = (iota((slots, spread), 0) == (iota((slots, spread), 1) & (slots - 1))).astype(f32).astype(bf16)
    stacked = jnp.concatenate([tile_of, lane_of, levels_ref[...]], axis=1).astype(f32).astype(bf16)
    wide = lax.dot_general(stacked, repeat, (((0,), (0,)), ((), ())), preferred_element_type=f32)
    own = lax.shift_right_logical(iota((8, spread), 1), 5) == iota((8, spread), 0)
    lane_ids = iota((lanes, spread), 0).astype(f32)
    for block in range(queries // 8):
        rows = slice(8 * block, 8 * block + 8)
        tile_now = wide[rows]
        lane_now = wide[queries + 8 * block : queries + 8 * block + 8]
        level_now = wide[2 * queries + 8 * block : 2 * queries + 8 * block + 8]
        lane_row = jnp.sum(jnp.where(own, lane_now, 0.0), axis=0, keepdims=True)
        level_own = jnp.where(own, level_now, 0.0)
        hot = jnp.where(lane_ids == lane_row, 1.0, 0.0).astype(bf16)
        parts = [jnp.where(tile_now == float(t), level_own, 0.0) for t in range(tiles)]
        totals = dot_nt(jnp.concatenate(parts, axis=0).astype(bf16), hot)
        for t in range(tiles):
            query_ref[rows, t * lanes : (t + 1) * lanes] = totals[8 * t : 8 * t + 8] * f32(0.01)
    place = iota((docs, queries), 0) + lax.axis_index("doc") * docs
    member = ids_ref[0:1, :] == place
    for j in range(1, ids_ref.shape[0]):
        member = member | (ids_ref[j : j + 1, :] == place)
    member = jnp.where(member, 1.0, 0.0).astype(bf16)
    wanted = iota((3 * queries, queries), 0)
    doubled = lax.shift_right_logical(wanted - queries, 3) * 4 + (wanted & 3)
    source = jnp.where(wanted < queries, wanted, doubled)
    pick = jnp.where(source == iota((3 * queries, queries), 1), 1.0, 0.0).astype(bf16)
    masks = dot_nt(pick, member)
    mask = masks[:queries]
    mask_ref[...] = masks[queries:].astype(bf16)
    copy.wait()
    scores = dot_nt(query_ref[...].astype(bf16), postings_ref[...])
    chosen = jnp.sum(scores * mask, axis=0, keepdims=True)
    high = chosen.astype(bf16).astype(f32)
    low = chosen - high
    steps = docs // lanes
    pieces = [x[:, i * lanes : (i + 1) * lanes] for x in (high, low) for i in range(steps)]
    tail = jnp.concatenate(pieces, axis=0).astype(bf16)
    for g in range(queries // 8):
        send_ref[g, :, 0:docs] = scores[8 * g : 8 * g + 8].astype(bf16)
        send_ref[g, :, docs : docs + lanes] = tail


def feedback_round(received_ref, mask_ref, postings_ref, first_ref, send_ref):
    groups = received_ref.shape[0]
    docs, width = postings_ref.shape
    total = received_ref[0].astype(f32)
    for g in range(1, groups):
        total = total + received_ref[g].astype(f32)
    first_ref[...] = total[:, 0:docs]
    steps = docs // lanes
    tail = total[:, docs : docs + lanes]
    weight = jnp.concatenate([tail[i : i + 1] + tail[steps + i : steps + i + 1] for i in range(steps)], axis=1)
    weight = weight.astype(bf16).astype(f32)
    mixing = (mask_ref[...].astype(f32) * weight).astype(bf16)
    postings = postings_ref[...]
    left = jnp.dot(mixing, postings[:, 0:half], preferred_element_type=f32)
    right = jnp.dot(mixing, postings[:, half:width], preferred_element_type=f32)
    sums = jnp.dot(mixing, jnp.ones((docs, lanes), bf16), preferred_element_type=f32)
    high = sums.astype(bf16).astype(f32)
    lane = iota(sums.shape, 1)
    sums = jnp.where(lane == 0, high, jnp.where(lane == 1, sums - high, 0.0))
    right = jnp.concatenate([right, sums], axis=1)
    upper = iota((8, half), 0) < 4
    for c in range(send_ref.shape[0]):
        rows = slice(8 * c, 8 * c + 8)
        send_ref[c] = jnp.where(upper, left[rows], right[rows]).astype(bf16)


def expand(received_ref, query_ref, out_ref):
    chunk, width = out_ref.shape
    total = received_ref[0].astype(f32)
    for d in range(1, received_ref.shape[0]):
        total = total + received_ref[d].astype(f32)
    rest = width - half
    weight = total[chunk:, rest : rest + 1] + total[chunk:, rest + 1 : rest + 2]
    doc = lax.axis_index("doc")
    pair = query_ref[pl.ds(pl.multiple_of(lax.shift_right_logical(doc, 1) * 8, 8), 8), :]
    mine = jnp.where((doc & 1) == 0, pair[:chunk], pair[chunk:])
    left = mine[:, :half] + expansion_weight * total[:chunk] / weight
    right = mine[:, half:] + expansion_weight * total[chunk:, :rest] / weight
    out_ref[:, 0:half] = left.astype(bf16)
    out_ref[:, half:width] = right.astype(bf16)


def per_device(postings, query_terms, query_levels, feedback_ids):
    docs, width = postings.shape
    queries = query_terms.shape[0]
    groups = lax.axis_size("term")
    blocks = lax.axis_size("doc")
    group = queries // groups
    chunk = queries // blocks
    shape = jax.ShapeDtypeStruct
    send, mask, query = pl.pallas_call(
        first_round,
        out_shape=(
            shape((groups, group, docs + lanes), bf16),
            shape((2 * queries, docs), bf16),
            shape((queries, width), f32),
        ),
        in_specs=[VMEM, VMEM, VMEM, pl.BlockSpec(memory_space=pltpu.HBM)],
        out_specs=(VMEM, VMEM, VMEM),
        scratch_shapes=[pltpu.VMEM((docs, width), bf16), pltpu.SemaphoreType.DMA],
        compiler_params=pltpu.CompilerParams(vmem_limit_bytes=32 << 20),
        name="first_round",
    )(query_terms.T, query_levels.T, feedback_ids.T, pltpu.with_memory_space_constraint(postings, pltpu.HBM))
    received = lax.all_to_all(send, "term", 0, 0)
    first, send = pl.pallas_call(
        feedback_round,
        out_shape=(shape((group, docs), f32), shape((blocks, 8, half), bf16)),
        in_specs=[VMEM] * 3,
        out_specs=(VMEM, VMEM),
        compiler_params=pltpu.CompilerParams(vmem_limit_bytes=32 << 20),
        name="feedback_round",
    )(received, mask, postings)
    received = lax.all_to_all(send, "doc", 0, 0)
    expanded = pl.pallas_call(
        expand,
        out_shape=shape((chunk, width), bf16),
        in_specs=[VMEM] * 2,
        out_specs=VMEM,
        compiler_params=pltpu.CompilerParams(vmem_limit_bytes=32 << 20),
        name="expand",
    )(received, query)
    gathered = lax.all_to_all(jnp.broadcast_to(expanded[None], (blocks, chunk, width)), "doc", 0, 0)
    partial = dot_nt(gathered.reshape(queries, width), postings).astype(bf16)
    partial = lax.all_to_all(partial.reshape(groups, group, docs), "term", 0, 0)
    return first, jnp.sum(partial.astype(f32), axis=0)


def solution(mesh):
    return jax.shard_map(
        per_device,
        mesh=mesh,
        in_specs=(P("doc", "term"), P(), P(), P()),
        out_specs=(P("term", "doc"), P("term", "doc")),
        check_vma=False,
    )
```

time: 420 us -> 91.1 us (0.22)
  the two profiles are of different devices: /device:TPU:6 before, /device:TPU:33 now
where the time goes in v2:
time: 91.1 us; the launch traced here: 90.6 us
  blocking collectives  82.1 us (90%)
  Pallas kernels  3.87 us (4%)
  local copies, waits for them, and re-layouts  2.51 us (3%)
    all_to_all x1, blocking collectives, per_device(): received = lax.all_to_all(send, 'term', 0, 0)  28.3 us
    all_to_all x1, blocking collectives, per_device(): received = lax.all_to_all(send, 'doc', 0, 0)  20.7 us
    all_to_all x1, blocking collectives, per_device(): partial = lax.all_to_all(partial.reshape(groups, group, docs), 'term', 0, 0)  18.4 us
    all_to_all x1, blocking collectives, per_device(): lax.all_to_all(jnp.broadcast_to(expanded[None], (blocks, chunk, width)),...  14.7 us
    pallas_call x1, Pallas kernels, per_device(): pl.pallas_call(first_round, out_shape=(shape((groups, group, docs + lanes...  2.35 us
    unnamed x8, local copies, waits for them, and re-layouts  2.27 us

profile of v2, /device:TPU:33, one launch (start us, length us, event | category | flops | bytes accessed | tf_op | source)
XLA Modules:
  0.0 90.6 jit_solution(13567405316524813186)
XLA Ops:
  0.6 0.0 copy-start
  0.6 0.0 copy-start.1
  0.7 0.8 copy-done.1
  1.5 0.0 copy-start.2
  1.5 0.7 copy-done.2
  2.2 0.0 copy-start.3
  2.2 0.7 copy-done.3
  2.9 2.3 %first_round.1 = (bf16[16,8,640]{2,1,0:T(8,128)(2,1)S(1)}, bf16[256,512]{1,0:T(8,128)(2,1)S(1)}, f32[128,1920]{1,0:T(8,128)S(1)}) custom-call(s32[32,128]{1,0:T(8,128)S(1)} %bitcast.7, s32[32,128]{1,0:T(8,128)S(1)} %bitcast.8, s32[10,128]{1,0:T(8,128)S(1)} %bitcast.9, bf16[512,1920]{1,0:T(8,128)(2,1)} %postings_ref.1), custom_call_target="tpu_custom_call" | custom-call | tf_op jit(solution)/shard_map/first_round/pallas_call | solution.py:127
  5.3 28.3 %all_to_all.20.received_ref = bf16[16,8,640]{2,1,0:T(8,128)(2,1)S(1)} all-to-all(bf16[16,8,640]{2,1,0:T(8,128)(2,1)S(1)} %get-tuple-element.7), channel_id=1, replica_groups=mesh['term'=16,'doc'=32] {'term'}, dimensions={0} | all-to-all | bytes 327680 | tf_op jit(solution)/shard_map/all_to_all | solution.py:140
  33.6 0.0 copy-done
  33.6 1.3 %feedback_round.1 = (f32[8,512]{1,0:T(8,128)}, bf16[32,8,1024]{2,1,0:T(8,128)(2,1)S(1)}) custom-call(bf16[16,8,640]{2,1,0:T(8,128)(2,1)S(1)} %all_to_all.20.received_ref, bf16[256,512]{1,0:T(8,128)(2,1)S(1)} %get-tuple-element.8.mask_ref, bf16[512,1920]{1,0:T(8,128)(2,1)S(1)} %copy-done), custom_call_target="tpu_custom_call" | custom-call | tf_op jit(solution)/shard_map/feedback_round/pallas_call | solution.py:141
  34.9 20.7 %all_to_all.21.received_ref = bf16[32,8,1024]{2,1,0:T(8,128)(2,1)S(1)} all-to-all(bf16[32,8,1024]{2,1,0:T(8,128)(2,1)S(1)} %get-tuple-element.10), channel_id=1, replica_groups=mesh['term'=16,'doc'=32] {'doc'}, dimensions={0} | all-to-all | bytes 1048576 | tf_op jit(solution)/shard_map/all_to_all | solution.py:149
  55.6 0.2 expand.1
  55.8 0.1 broadcast_in_dim.2
  56.0 14.7 %all_to_all.22 = bf16[32,4,1920]{2,1,0:T(4,128)(2,1)S(1)} all-to-all(bf16[32,4,1920]{2,1,0:T(4,128)(2,1)S(1)} %broadcast_in_dim.2), channel_id=1, replica_groups=mesh['term'=16,'doc'=32] {'doc'}, dimensions={0} | all-to-all | bytes 983040 | tf_op jit(solution)/shard_map/all_to_all | solution.py:158
  70.7 0.1 reshape.11
  70.8 0.8 fusion
  71.6 18.4 %all_to_all.23 = bf16[16,8,512]{2,1,0:T(8,128)(2,1)S(1)} all-to-all(bf16[16,8,512]{2,1,0:T(8,128)(2,1)S(1)} %fusion), channel_id=1, replica_groups=mesh['term'=16,'doc'=32] {'term'}, dimensions={0} | all-to-all | bytes 262144 | tf_op jit(solution)/shard_map/all_to_all | solution.py:160
  90.0 0.6 convert_reduce_fusion
Async XLA Ops:
  0.6 32.9 %copy-start = (bf16[512,1920]{1,0:T(8,128)(2,1)S(1)}, bf16[512,1920]{1,0:T(8,128)(2,1)}, u32[]{:S(2)}) copy-start(bf16[512,1920]{1,0:T(8,128)(2,1)} %postings_ref.1) | copy-start | bytes 5898244
  0.6 0.9 copy-start.1
  1.5 0.7 copy-start.2
  2.2 0.7 copy-start.3

commit v3 on v2

--- a/solution.py
+++ b/solution.py
@@ -21,10 +21,18 @@
     return lax.broadcasted_iota(jnp.int32, shape, axis)
 
 
-def first_round(terms_ref, levels_ref, ids_ref, postings_hbm, send_ref, mask_ref, query_ref,
-                postings_ref, sem):
-    copy = pltpu.make_async_copy(postings_hbm, postings_ref, sem)
-    copy.start()
+def first_round(terms_hbm, levels_hbm, ids_hbm, postings_hbm, send_ref, mask_ref, query_ref,
+                terms_ref, levels_ref, ids_ref, postings_ref, sems):
+    copies = [
+        pltpu.make_async_copy(source, target, sems.at[i])
+        for i, (source, target) in enumerate(
+            ((terms_hbm, terms_ref), (levels_hbm, levels_ref), (ids_hbm, ids_ref), (postings_hbm, postings_ref))
+        )
+    ]
+    for copy in copies:
+        copy.start()
+    copies[0].wait()
+    copies[1].wait()
     slots, queries = terms_ref.shape
     docs, width = postings_ref.shape
     tiles = width // lanes
@@ -49,6 +57,7 @@
         totals = dot_nt(jnp.concatenate(parts, axis=0).astype(bf16), hot)
         for t in range(tiles):
             query_ref[rows, t * lanes : (t + 1) * lanes] = totals[8 * t : 8 * t + 8] * f32(0.01)
+    copies[2].wait()
     place = iota((docs, queries), 0) + lax.axis_index("doc") * docs
     member = ids_ref[0:1, :] == place
     for j in range(1, ids_ref.shape[0]):
@@ -61,7 +70,7 @@
     masks = dot_nt(pick, member)
     mask = masks[:queries]
     mask_ref[...] = masks[queries:].astype(bf16)
-    copy.wait()
+    copies[3].wait()
     scores = dot_nt(query_ref[...].astype(bf16), postings_ref[...])
     chosen = jnp.sum(scores * mask, axis=0, keepdims=True)
     high = chosen.astype(bf16).astype(f32)
@@ -131,12 +140,21 @@
             shape((2 * queries, docs), bf16),
             shape((queries, width), f32),
         ),
-        in_specs=[VMEM, VMEM, VMEM, pl.BlockSpec(memory_space=pltpu.HBM)],
+        in_specs=[pl.BlockSpec(memory_space=pltpu.HBM)] * 4,
         out_specs=(VMEM, VMEM, VMEM),
-        scratch_shapes=[pltpu.VMEM((docs, width), bf16), pltpu.SemaphoreType.DMA],
+        scratch_shapes=[
+            pltpu.VMEM(query_terms.shape[::-1], jnp.int32),
+            pltpu.VMEM(query_levels.shape[::-1], jnp.int32),
+            pltpu.VMEM(feedback_ids.shape[::-1], jnp.int32),
+            pltpu.VMEM((docs, width), bf16),
+            pltpu.SemaphoreType.DMA((4,)),
+        ],
         compiler_params=pltpu.CompilerParams(vmem_limit_bytes=32 << 20),
         name="first_round",
-    )(query_terms.T, query_levels.T, feedback_ids.T, pltpu.with_memory_space_constraint(postings, pltpu.HBM))
+    )(*(
+        pltpu.with_memory_space_constraint(x, pltpu.HBM)
+        for x in (query_terms.T, query_levels.T, feedback_ids.T, postings)
+    ))
     received = lax.all_to_all(send, "term", 0, 0)
     first, send = pl.pallas_call(
         feedback_round,

time: 91.1 us -> 89.2 us (0.979)
  local copies, waits for them, and re-layouts: 2.51 us -> 0.25 us
    unnamed x8 -> x2, local copies, waits for them, and re-layouts: 2.27 us -> 0.01 us
where the time goes in v3:
time: 89.2 us; the launch traced here: 88.9 us
  blocking collectives  82.1 us (92%)
  Pallas kernels  4.47 us (5%)
    all_to_all x1, blocking collectives, per_device(): received = lax.all_to_all(send, 'term', 0, 0)  28.2 us
    all_to_all x1, blocking collectives, per_device(): received = lax.all_to_all(send, 'doc', 0, 0)  20.8 us
    all_to_all x1, blocking collectives, per_device(): partial = lax.all_to_all(partial.reshape(groups, group, docs), 'term', 0, 0)  18.4 us
    all_to_all x1, blocking collectives, per_device(): lax.all_to_all(jnp.broadcast_to(expanded[None], (blocks, chunk, width)),...  14.7 us
    pallas_call x1, Pallas kernels, per_device(): pl.pallas_call(first_round, out_shape=(shape((groups, group, docs + lanes...  2.95 us

profile of v3, /device:TPU:33, one launch (start us, length us, event | category | flops | bytes accessed | tf_op | source)
XLA Modules:
  0.0 88.9 jit_solution(17286188009494338160)
XLA Ops:
  0.6 0.0 copy-start
  0.6 3.0 %first_round.1 = (bf16[16,8,640]{2,1,0:T(8,128)(2,1)S(1)}, bf16[256,512]{1,0:T(8,128)(2,1)S(1)}, f32[128,1920]{1,0:T(8,128)S(1)}) custom-call(s32[32,128]{1,0:T(8,128)} %bitcast.7, s32[32,128]{1,0:T(8,128)} %bitcast.8, s32[10,128]{1,0:T(8,128)} %bitcast.9, bf16[512,1920]{1,0:T(8,128)(2,1)} %postings_ref.1), custom_call_target="tpu_custom_call" | custom-call | tf_op jit(solution)/shard_map/first_round/pallas_call | solution.py:136
  3.6 28.2 %all_to_all.20.received_ref = bf16[16,8,640]{2,1,0:T(8,128)(2,1)S(1)} all-to-all(bf16[16,8,640]{2,1,0:T(8,128)(2,1)S(1)} %get-tuple-element.7), channel_id=1, replica_groups=mesh['term'=16,'doc'=32] {'term'}, dimensions={0} | all-to-all | bytes 327680 | tf_op jit(solution)/shard_map/all_to_all | solution.py:158
  31.8 0.0 copy-done
  31.8 1.3 %feedback_round.1 = (f32[8,512]{1,0:T(8,128)}, bf16[32,8,1024]{2,1,0:T(8,128)(2,1)S(1)}) custom-call(bf16[16,8,640]{2,1,0:T(8,128)(2,1)S(1)} %all_to_all.20.received_ref, bf16[256,512]{1,0:T(8,128)(2,1)S(1)} %get-tuple-element.8.mask_ref, bf16[512,1920]{1,0:T(8,128)(2,1)S(1)} %copy-done), custom_call_target="tpu_custom_call" | custom-call | tf_op jit(solution)/shard_map/feedback_round/pallas_call | solution.py:159
  33.2 20.8 %all_to_all.21.received_ref = bf16[32,8,1024]{2,1,0:T(8,128)(2,1)S(1)} all-to-all(bf16[32,8,1024]{2,1,0:T(8,128)(2,1)S(1)} %get-tuple-element.10), channel_id=1, replica_groups=mesh['term'=16,'doc'=32] {'doc'}, dimensions={0} | all-to-all | bytes 1048576 | tf_op jit(solution)/shard_map/all_to_all | solution.py:167
  54.0 0.2 expand.1
  54.2 0.1 broadcast_in_dim.2
  54.3 14.7 %all_to_all.22 = bf16[32,4,1920]{2,1,0:T(4,128)(2,1)S(1)} all-to-all(bf16[32,4,1920]{2,1,0:T(4,128)(2,1)S(1)} %broadcast_in_dim.2), channel_id=1, replica_groups=mesh['term'=16,'doc'=32] {'doc'}, dimensions={0} | all-to-all | bytes 983040 | tf_op jit(solution)/shard_map/all_to_all | solution.py:176
  69.0 0.1 reshape.11
  69.2 0.8 fusion
  69.9 18.4 %all_to_all.23 = bf16[16,8,512]{2,1,0:T(8,128)(2,1)S(1)} all-to-all(bf16[16,8,512]{2,1,0:T(8,128)(2,1)S(1)} %fusion), channel_id=1, replica_groups=mesh['term'=16,'doc'=32] {'term'}, dimensions={0} | all-to-all | bytes 262144 | tf_op jit(solution)/shard_map/all_to_all | solution.py:178
  88.3 0.6 convert_reduce_fusion
Async XLA Ops:
  0.6 31.2 %copy-start = (bf16[512,1920]{1,0:T(8,128)(2,1)S(1)}, bf16[512,1920]{1,0:T(8,128)(2,1)}, u32[]{:S(2)}) copy-start(bf16[512,1920]{1,0:T(8,128)(2,1)} %postings_ref.1) | copy-start | bytes 5898244

commit v4 on v3

--- a/solution.py
+++ b/solution.py
@@ -7,7 +7,6 @@
 
 expansion_weight = 0.25
 lanes = 128
-half = 1024
 f32 = jnp.float32
 bf16 = jnp.bfloat16
 VMEM = pl.BlockSpec(memory_space=pltpu.VMEM)
@@ -21,14 +20,11 @@
     return lax.broadcasted_iota(jnp.int32, shape, axis)
 
 
-def first_round(terms_hbm, levels_hbm, ids_hbm, postings_hbm, send_ref, mask_ref, query_ref,
-                terms_ref, levels_ref, ids_ref, postings_ref, sems):
-    copies = [
-        pltpu.make_async_copy(source, target, sems.at[i])
-        for i, (source, target) in enumerate(
-            ((terms_hbm, terms_ref), (levels_hbm, levels_ref), (ids_hbm, ids_ref), (postings_hbm, postings_ref))
-        )
-    ]
+def first_round(terms_hbm, levels_hbm, ids_hbm, postings_hbm, send_ref, mask_ref, query_ref, postings_ref,
+                terms_ref, levels_ref, ids_ref, sems):
+    pairs = [(terms_hbm, terms_ref), (levels_hbm, levels_ref), (ids_hbm, ids_ref)]
+    pairs.append((postings_hbm, postings_ref))
+    copies = [pltpu.make_async_copy(source, target, sems.at[i]) for i, (source, target) in enumerate(pairs)]
     for copy in copies:
         copy.start()
     copies[0].wait()
@@ -63,24 +59,17 @@
     for j in range(1, ids_ref.shape[0]):
         member = member | (ids_ref[j : j + 1, :] == place)
     member = jnp.where(member, 1.0, 0.0).astype(bf16)
-    wanted = iota((3 * queries, queries), 0)
-    doubled = lax.shift_right_logical(wanted - queries, 3) * 4 + (wanted & 3)
-    source = jnp.where(wanted < queries, wanted, doubled)
-    pick = jnp.where(source == iota((3 * queries, queries), 1), 1.0, 0.0).astype(bf16)
-    masks = dot_nt(pick, member)
-    mask = masks[:queries]
-    mask_ref[...] = masks[queries:].astype(bf16)
+    same = jnp.where(iota((queries, queries), 0) == iota((queries, queries), 1), 1.0, 0.0).astype(bf16)
+    mask = dot_nt(same, member)
+    mask_ref[...] = mask.astype(bf16)
     copies[3].wait()
     scores = dot_nt(query_ref[...].astype(bf16), postings_ref[...])
     chosen = jnp.sum(scores * mask, axis=0, keepdims=True)
-    high = chosen.astype(bf16).astype(f32)
-    low = chosen - high
-    steps = docs // lanes
-    pieces = [x[:, i * lanes : (i + 1) * lanes] for x in (high, low) for i in range(steps)]
-    tail = jnp.concatenate(pieces, axis=0).astype(bf16)
+    tail = jnp.concatenate([chosen[:, i : i + lanes] for i in range(0, docs, lanes)], axis=0).astype(bf16)
     for g in range(queries // 8):
-        send_ref[g, :, 0:docs] = scores[8 * g : 8 * g + 8].astype(bf16)
-        send_ref[g, :, docs : docs + lanes] = tail
+        send_ref[g, :, 0:docs] = scores[8 * g : 8 * g + 4].astype(bf16)
+        send_ref[g, :, docs : 2 * docs] = scores[8 * g + 4 : 8 * g + 8].astype(bf16)
+        send_ref[g, :, 2 * docs :] = tail
 
 
 def feedback_round(received_ref, mask_ref, postings_ref, first_ref, send_ref):
@@ -89,24 +78,22 @@
     total = received_ref[0].astype(f32)
     for g in range(1, groups):
         total = total + received_ref[g].astype(f32)
-    first_ref[...] = total[:, 0:docs]
-    steps = docs // lanes
-    tail = total[:, docs : docs + lanes]
-    weight = jnp.concatenate([tail[i : i + 1] + tail[steps + i : steps + i + 1] for i in range(steps)], axis=1)
+    first_ref[0:4] = total[:, 0:docs]
+    first_ref[4:8] = total[:, docs : 2 * docs]
+    tail = total[:, 2 * docs :]
+    weight = jnp.concatenate([tail[i : i + 1] for i in range(docs // lanes)], axis=1)
     weight = weight.astype(bf16).astype(f32)
     mixing = (mask_ref[...].astype(f32) * weight).astype(bf16)
     postings = postings_ref[...]
-    left = jnp.dot(mixing, postings[:, 0:half], preferred_element_type=f32)
-    right = jnp.dot(mixing, postings[:, half:width], preferred_element_type=f32)
+    numerator = jnp.dot(mixing, postings, preferred_element_type=f32)
     sums = jnp.dot(mixing, jnp.ones((docs, lanes), bf16), preferred_element_type=f32)
     high = sums.astype(bf16).astype(f32)
     lane = iota(sums.shape, 1)
     sums = jnp.where(lane == 0, high, jnp.where(lane == 1, sums - high, 0.0))
-    right = jnp.concatenate([right, sums], axis=1)
-    upper = iota((8, half), 0) < 4
     for c in range(send_ref.shape[0]):
-        rows = slice(8 * c, 8 * c + 8)
-        send_ref[c] = jnp.where(upper, left[rows], right[rows]).astype(bf16)
+        rows = slice(4 * c, 4 * c + 4)
+        send_ref[c, :, 0:width] = numerator[rows].astype(bf16)
+        send_ref[c, :, width : width + lanes] = sums[rows].astype(bf16)
 
 
 def expand(received_ref, query_ref, out_ref):
@@ -114,15 +101,11 @@
     total = received_ref[0].astype(f32)
     for d in range(1, received_ref.shape[0]):
         total = total + received_ref[d].astype(f32)
-    rest = width - half
-    weight = total[chunk:, rest : rest + 1] + total[chunk:, rest + 1 : rest + 2]
+    weight = total[:, width : width + 1] + total[:, width + 1 : width + 2]
     doc = lax.axis_index("doc")
     pair = query_ref[pl.ds(pl.multiple_of(lax.shift_right_logical(doc, 1) * 8, 8), 8), :]
     mine = jnp.where((doc & 1) == 0, pair[:chunk], pair[chunk:])
-    left = mine[:, :half] + expansion_weight * total[:chunk] / weight
-    right = mine[:, half:] + expansion_weight * total[chunk:, :rest] / weight
-    out_ref[:, 0:half] = left.astype(bf16)
-    out_ref[:, half:width] = right.astype(bf16)
+    out_ref[...] = (mine + expansion_weight * total[:, :width] / weight).astype(bf16)
 
 
 def per_device(postings, query_terms, query_levels, feedback_ids):
@@ -133,20 +116,20 @@
     group = queries // groups
     chunk = queries // blocks
     shape = jax.ShapeDtypeStruct
-    send, mask, query = pl.pallas_call(
+    send, mask, query, postings = pl.pallas_call(
         first_round,
         out_shape=(
-            shape((groups, group, docs + lanes), bf16),
-            shape((2 * queries, docs), bf16),
+            shape((groups, group // 2, 2 * docs + lanes), bf16),
+            shape((queries, docs), bf16),
             shape((queries, width), f32),
+            shape((docs, width), bf16),
         ),
         in_specs=[pl.BlockSpec(memory_space=pltpu.HBM)] * 4,
-        out_specs=(VMEM, VMEM, VMEM),
+        out_specs=(VMEM,) * 4,
         scratch_shapes=[
             pltpu.VMEM(query_terms.shape[::-1], jnp.int32),
             pltpu.VMEM(query_levels.shape[::-1], jnp.int32),
             pltpu.VMEM(feedback_ids.shape[::-1], jnp.int32),
-            pltpu.VMEM((docs, width), bf16),
             pltpu.SemaphoreType.DMA((4,)),
         ],
         compiler_params=pltpu.CompilerParams(vmem_limit_bytes=32 << 20),
@@ -158,7 +141,7 @@
     received = lax.all_to_all(send, "term", 0, 0)
     first, send = pl.pallas_call(
         feedback_round,
-        out_shape=(shape((group, docs), f32), shape((blocks, 8, half), bf16)),
+        out_shape=(shape((group, docs), f32), shape((blocks, chunk, width + lanes), bf16)),
         in_specs=[VMEM] * 3,
         out_specs=(VMEM, VMEM),
         compiler_params=pltpu.CompilerParams(vmem_limit_bytes=32 << 20),

time: 89.2 us -> 88 us (0.987)
  no operation moved by 1% of the time
where the time goes in v4:
time: 88 us; the launch traced here: 87.7 us
  blocking collectives  81.4 us (93%)
  Pallas kernels  3.95 us (4%)
    all_to_all x1, blocking collectives, per_device(): received = lax.all_to_all(send, 'term', 0, 0)  27.4 us
    all_to_all x1, blocking collectives, per_device(): received = lax.all_to_all(send, 'doc', 0, 0)  21.4 us
    all_to_all x1, blocking collectives, per_device(): partial = lax.all_to_all(partial.reshape(groups, group, docs), 'term', 0, 0)  17.8 us
    all_to_all x1, blocking collectives, per_device(): lax.all_to_all(jnp.broadcast_to(expanded[None], (blocks, chunk, width)),...  14.7 us
    pallas_call x1, Pallas kernels, per_device(): pl.pallas_call(first_round, out_shape=(shape((groups, group // 2, 2 * doc...  2.74 us

profile of v4, /device:TPU:33, one launch (start us, length us, event | category | flops | bytes accessed | tf_op | source)
XLA Modules:
  0.0 87.7 jit_solution(2944077499452385913)
XLA Ops:
  0.6 2.7 %first_round.1 = (bf16[16,4,1152]{2,1,0:T(4,128)(2,1)S(1)}, bf16[128,512]{1,0:T(8,128)(2,1)S(1)}, f32[128,1920]{1,0:T(8,128)S(1)}, bf16[512,1920]{1,0:T(8,128)(2,1)S(1)}) custom-call(s32[32,128]{1,0:T(8,128)} %bitcast.7, s32[32,128]{1,0:T(8,128)} %bitcast.8, s32[10,128]{1,0:T(8,128)} %bitcast.9, bf16[512,1920]{1,0:T(8,128)(2,1)} %postings_hbm.1), custom_call_target="tpu_custom_call" | custom-call | tf_op jit(solution)/shard_map/first_round/pallas_call | solution.py:119
  3.4 27.4 %all_to_all.20.received_ref = bf16[16,4,1152]{2,1,0:T(4,128)(2,1)S(1)} all-to-all(bf16[16,4,1152]{2,1,0:T(4,128)(2,1)S(1)} %get-tuple-element.8), channel_id=1, replica_groups=mesh['term'=16,'doc'=32] {'term'}, dimensions={0} | all-to-all | bytes 294912 | tf_op jit(solution)/shard_map/all_to_all | solution.py:141
  30.8 1.0 %feedback_round.1 = (f32[8,512]{1,0:T(8,128)}, bf16[32,4,2048]{2,1,0:T(4,128)(2,1)S(1)}) custom-call(bf16[16,4,1152]{2,1,0:T(4,128)(2,1)S(1)} %all_to_all.20.received_ref, bf16[128,512]{1,0:T(8,128)(2,1)S(1)} %get-tuple-element.9.mask_ref, bf16[512,1920]{1,0:T(8,128)(2,1)S(1)} %get-tuple-element.10.postings_ref), custom_call_target="tpu_custom_call" | custom-call | tf_op jit(solution)/shard_map/feedback_round/pallas_call | solution.py:142
  31.8 21.4 %all_to_all.21.received_ref = bf16[32,4,2048]{2,1,0:T(4,128)(2,1)S(1)} all-to-all(bf16[32,4,2048]{2,1,0:T(4,128)(2,1)S(1)} %get-tuple-element.12), channel_id=1, replica_groups=mesh['term'=16,'doc'=32] {'doc'}, dimensions={0} | all-to-all | bytes 1048576 | tf_op jit(solution)/shard_map/all_to_all | solution.py:150
  53.3 0.2 expand.1
  53.5 0.1 broadcast_in_dim.2
  53.6 14.7 %all_to_all.22 = bf16[32,4,1920]{2,1,0:T(4,128)(2,1)S(1)} all-to-all(bf16[32,4,1920]{2,1,0:T(4,128)(2,1)S(1)} %broadcast_in_dim.2), channel_id=1, replica_groups=mesh['term'=16,'doc'=32] {'doc'}, dimensions={0} | all-to-all | bytes 983040 | tf_op jit(solution)/shard_map/all_to_all | solution.py:159
  68.3 0.1 reshape.11
  68.4 0.8 fusion
  69.2 17.8 %all_to_all.23 = bf16[16,8,512]{2,1,0:T(8,128)(2,1)S(1)} all-to-all(bf16[16,8,512]{2,1,0:T(8,128)(2,1)S(1)} %fusion), channel_id=1, replica_groups=mesh['term'=16,'doc'=32] {'term'}, dimensions={0} | all-to-all | bytes 262144 | tf_op jit(solution)/shard_map/all_to_all | solution.py:161
  87.1 0.6 convert_reduce_fusion

commit v5 on v4

--- a/solution.py
+++ b/solution.py
@@ -1,3 +1,5 @@
+import functools
+
 import jax
 import jax.numpy as jnp
 from jax import lax
@@ -7,6 +9,7 @@
 
 expansion_weight = 0.25
 lanes = 128
+first_top = 32 * 2.55 * 3.0 * 1.001
 f32 = jnp.float32
 bf16 = jnp.bfloat16
 VMEM = pl.BlockSpec(memory_space=pltpu.VMEM)
@@ -18,6 +21,18 @@
 
 def iota(shape, axis):
     return lax.broadcasted_iota(jnp.int32, shape, axis)
+
+
+def encode(x, top):
+    root = jnp.sqrt(jnp.sqrt(jnp.sqrt(x * f32(1.0 / top))))
+    return (jnp.round(root * f32(65535.0)).astype(jnp.int32) - 32768).astype(jnp.int16)
+
+
+def decode(codes, top):
+    root = (codes.astype(jnp.int32).astype(f32) + f32(32768.0)) * f32(top**0.125 / 65535.0)
+    square = root * root
+    fourth = square * square
+    return fourth * fourth
 
 
 def first_round(terms_hbm, levels_hbm, ids_hbm, postings_hbm, send_ref, mask_ref, query_ref, postings_ref,
@@ -65,22 +80,21 @@
     copies[3].wait()
     scores = dot_nt(query_ref[...].astype(bf16), postings_ref[...])
     chosen = jnp.sum(scores * mask, axis=0, keepdims=True)
-    tail = jnp.concatenate([chosen[:, i : i + lanes] for i in range(0, docs, lanes)], axis=0).astype(bf16)
+    tail = jnp.concatenate([chosen[:, i : i + lanes] for i in range(0, docs, lanes)], axis=0)
+    tail = encode(tail, first_top)
+    codes = encode(scores, first_top)
     for g in range(queries // 8):
-        send_ref[g, :, 0:docs] = scores[8 * g : 8 * g + 4].astype(bf16)
-        send_ref[g, :, docs : 2 * docs] = scores[8 * g + 4 : 8 * g + 8].astype(bf16)
+        send_ref[g, :, 0:docs] = codes[8 * g : 8 * g + 4]
+        send_ref[g, :, docs : 2 * docs] = codes[8 * g + 4 : 8 * g + 8]
         send_ref[g, :, 2 * docs :] = tail
 
 
-def feedback_round(received_ref, mask_ref, postings_ref, first_ref, send_ref):
+def feedback_round(received_ref, mask_ref, postings_ref, send_ref):
     groups = received_ref.shape[0]
     docs, width = postings_ref.shape
-    total = received_ref[0].astype(f32)
+    tail = decode(received_ref[0, :, 2 * docs :], first_top)
     for g in range(1, groups):
-        total = total + received_ref[g].astype(f32)
-    first_ref[0:4] = total[:, 0:docs]
-    first_ref[4:8] = total[:, docs : 2 * docs]
-    tail = total[:, 2 * docs :]
+        tail = tail + decode(received_ref[g, :, 2 * docs :], first_top)
     weight = jnp.concatenate([tail[i : i + 1] for i in range(docs // lanes)], axis=1)
     weight = weight.astype(bf16).astype(f32)
     mixing = (mask_ref[...].astype(f32) * weight).astype(bf16)
@@ -96,6 +110,21 @@
         send_ref[c, :, width : width + lanes] = sums[rows].astype(bf16)
 
 
+def totals(first_codes_ref, final_codes_ref, first_ref, final_ref, *, final_top):
+    groups, rows, docs = final_codes_ref.shape
+    folded = rows // 2
+    for side in range(2):
+        columns = slice(side * docs, (side + 1) * docs)
+        total = decode(first_codes_ref[0, :, columns], first_top)
+        for g in range(1, groups):
+            total = total + decode(first_codes_ref[g, :, columns], first_top)
+        first_ref[side * folded : (side + 1) * folded] = total
+    total = decode(final_codes_ref[0], final_top)
+    for g in range(1, groups):
+        total = total + decode(final_codes_ref[g], final_top)
+    final_ref[...] = total
+
+
 def expand(received_ref, query_ref, out_ref):
     chunk, width = out_ref.shape
     total = received_ref[0].astype(f32)
@@ -116,10 +145,11 @@
     group = queries // groups
     chunk = queries // blocks
     shape = jax.ShapeDtypeStruct
+    final_top = first_top + expansion_weight * 3.0 * 3.0 * 1.01 * width
     send, mask, query, postings = pl.pallas_call(
         first_round,
         out_shape=(
-            shape((groups, group // 2, 2 * docs + lanes), bf16),
+            shape((groups, group // 2, 2 * docs + lanes), jnp.int16),
             shape((queries, docs), bf16),
             shape((queries, width), f32),
             shape((docs, width), bf16),
@@ -138,15 +168,15 @@
         pltpu.with_memory_space_constraint(x, pltpu.HBM)
         for x in (query_terms.T, query_levels.T, feedback_ids.T, postings)
     ))
-    received = lax.all_to_all(send, "term", 0, 0)
-    first, send = pl.pallas_call(
+    first_codes = lax.all_to_all(send, "term", 0, 0)
+    send = pl.pallas_call(
         feedback_round,
-        out_shape=(shape((group, docs), f32), shape((blocks, chunk, width + lanes), bf16)),
+        out_shape=shape((blocks, chunk, width + lanes), bf16),
         in_specs=[VMEM] * 3,
-        out_specs=(VMEM, VMEM),
+        out_specs=VMEM,
         compiler_params=pltpu.CompilerParams(vmem_limit_bytes=32 << 20),
         name="feedback_round",
-    )(received, mask, postings)
+    )(first_codes, mask, postings)
     received = lax.all_to_all(send, "doc", 0, 0)
     expanded = pl.pallas_call(
         expand,
@@ -157,9 +187,16 @@
         name="expand",
     )(received, query)
     gathered = lax.all_to_all(jnp.broadcast_to(expanded[None], (blocks, chunk, width)), "doc", 0, 0)
-    partial = dot_nt(gathered.reshape(queries, width), postings).astype(bf16)
+    partial = encode(dot_nt(gathered.reshape(queries, width), postings), final_top)
     partial = lax.all_to_all(partial.reshape(groups, group, docs), "term", 0, 0)
-    return first, jnp.sum(partial.astype(f32), axis=0)
+    return pl.pallas_call(
+        functools.partial(totals, final_top=final_top),
+        out_shape=(shape((group, docs), f32),) * 2,
+        in_specs=[VMEM] * 2,
+        out_specs=(VMEM,) * 2,
+        compiler_params=pltpu.CompilerParams(vmem_limit_bytes=32 << 20),
+        name="totals",
+    )(first_codes, partial)
 
 
 def solution(mesh):

time: 88 us -> 88 us (level)
  no operation moved by 1% of the time
where the time goes in v5:
time: 88 us; the launch traced here: 87.7 us
  blocking collectives  81.4 us (93%)
  Pallas kernels  4.4 us (5%)
  matrix products  0.96 us (1%)
    all_to_all x1, blocking collectives, per_device(): first_codes = lax.all_to_all(send, 'term', 0, 0)  27.4 us
    all_to_all x1, blocking collectives, per_device(): received = lax.all_to_all(send, 'doc', 0, 0)  21.5 us
    all_to_all x1, blocking collectives, per_device(): partial = lax.all_to_all(partial.reshape(groups, group, docs), 'term', 0, 0)  17.8 us
    all_to_all x1, blocking collectives, per_device(): lax.all_to_all(jnp.broadcast_to(expanded[None], (blocks, chunk, width)),...  14.7 us
    pallas_call x1, Pallas kernels, per_device(): pl.pallas_call(first_round, out_shape=(shape((groups, group // 2, 2 * doc...  2.97 us

profile of v5, /device:TPU:33, one launch (start us, length us, event | category | flops | bytes accessed | tf_op | source)
XLA Modules:
  0.0 87.7 jit_solution(6049605469804274093)
XLA Ops:
  0.6 3.0 %first_round.1 = (s16[16,4,1152]{2,1,0:T(4,128)(2,1)S(1)}, bf16[128,512]{1,0:T(8,128)(2,1)S(1)}, f32[128,1920]{1,0:T(8,128)S(1)}, bf16[512,1920]{1,0:T(8,128)(2,1)S(1)}) custom-call(s32[32,128]{1,0:T(8,128)} %bitcast.7, s32[32,128]{1,0:T(8,128)} %bitcast.8, s32[10,128]{1,0:T(8,128)} %bitcast.9, bf16[512,1920]{1,0:T(8,128)(2,1)} %postings_hbm.1), custom_call_target="tpu_custom_call" | custom-call | tf_op jit(solution)/shard_map/first_round/pallas_call | solution.py:149
  3.6 27.4 %all_to_all.20.received_ref.first_codes_ref = s16[16,4,1152]{2,1,0:T(4,128)(2,1)S(1)} all-to-all(s16[16,4,1152]{2,1,0:T(4,128)(2,1)S(1)} %get-tuple-element.6), channel_id=1, replica_groups=mesh['term'=16,'doc'=32] {'term'}, dimensions={0} | all-to-all | bytes 294912 | tf_op jit(solution)/shard_map/all_to_all | solution.py:171
  31.0 0.5 feedback_round.1
  31.5 21.5 %all_to_all.21.received_ref = bf16[32,4,2048]{2,1,0:T(4,128)(2,1)S(1)} all-to-all(bf16[32,4,2048]{2,1,0:T(4,128)(2,1)S(1)} %feedback_round.1), channel_id=1, replica_groups=mesh['term'=16,'doc'=32] {'doc'}, dimensions={0} | all-to-all | bytes 1048576 | tf_op jit(solution)/shard_map/all_to_all | solution.py:180
  53.0 0.2 expand.1
  53.2 0.1 broadcast_in_dim.2
  53.3 14.7 %all_to_all.22 = bf16[32,4,1920]{2,1,0:T(4,128)(2,1)S(1)} all-to-all(bf16[32,4,1920]{2,1,0:T(4,128)(2,1)S(1)} %broadcast_in_dim.2), channel_id=1, replica_groups=mesh['term'=16,'doc'=32] {'doc'}, dimensions={0} | all-to-all | bytes 983040 | tf_op jit(solution)/shard_map/all_to_all | solution.py:189
  68.0 0.1 reshape.11
  68.2 1.0 %fusion.8 = s16[16,8,512]{2,1,0:T(8,128)(2,1)S(1)} fusion(bf16[128,1920]{1,0:T(8,128)(2,1)S(1)} %reshape.11, bf16[512,1920]{1,0:T(8,128)(2,1)S(1)} %get-tuple-element.8.postings_ref), kind=kOutput, calls=%fused_computation.9 | convolution fusion | flops 252051456 | bytes 2588672 | tf_op jit(solution)/shard_map/dot_general | solution.py:19
  69.1 17.8 %all_to_all.23.final_codes_ref = s16[16,8,512]{2,1,0:T(8,128)(2,1)S(1)} all-to-all(s16[16,8,512]{2,1,0:T(8,128)(2,1)S(1)} %fusion.8), channel_id=1, replica_groups=mesh['term'=16,'doc'=32] {'term'}, dimensions={0} | all-to-all | bytes 262144 | tf_op jit(solution)/shard_map/all_to_all | solution.py:191
  87.0 0.7 totals.1

commit v6 on v5

--- a/solution.py
+++ b/solution.py
@@ -24,8 +24,10 @@
 
 
 def encode(x, top):
-    root = jnp.sqrt(jnp.sqrt(jnp.sqrt(x * f32(1.0 / top))))
-    return (jnp.round(root * f32(65535.0)).astype(jnp.int32) - 32768).astype(jnp.int16)
+    root = jnp.maximum(x * f32(1.0 / top), f32(1e-37))
+    for _ in range(3):
+        root = root * lax.rsqrt(root)
+    return ((root * f32(65535.0) + f32(0.5)).astype(jnp.int32) - 32768).astype(jnp.int16)
 
 
 def decode(codes, top):
@@ -69,11 +71,12 @@
         for t in range(tiles):
             query_ref[rows, t * lanes : (t + 1) * lanes] = totals[8 * t : 8 * t + 8] * f32(0.01)
     copies[2].wait()
-    place = iota((docs, queries), 0) + lax.axis_index("doc") * docs
-    member = ids_ref[0:1, :] == place
-    for j in range(1, ids_ref.shape[0]):
-        member = member | (ids_ref[j : j + 1, :] == place)
-    member = jnp.where(member, 1.0, 0.0).astype(bf16)
+    place = (iota((docs, queries), 0) + lax.axis_index("doc") * docs).astype(jnp.int16)
+    ids = ids_ref[...].astype(jnp.int16)
+    member = ids[0:1, :] == place
+    for j in range(1, ids.shape[0]):
+        member = member | (ids[j : j + 1, :] == place)
+    member = jnp.where(member, jnp.ones((), bf16), jnp.zeros((), bf16))
     same = jnp.where(iota((queries, queries), 0) == iota((queries, queries), 1), 1.0, 0.0).astype(bf16)
     mask = dot_nt(same, member)
     mask_ref[...] = mask.astype(bf16)

time: 88 us -> 87.7 us (level)
  no operation moved by 1% of the time
where the time goes in v6:
time: 87.7 us; the launch traced here: 87.4 us
  blocking collectives  81.4 us (93%)
  Pallas kernels  4.15 us (5%)
  matrix products  0.89 us (1%)
    all_to_all x1, blocking collectives, per_device(): first_codes = lax.all_to_all(send, 'term', 0, 0)  27.4 us
    all_to_all x1, blocking collectives, per_device(): received = lax.all_to_all(send, 'doc', 0, 0)  21.4 us
    all_to_all x1, blocking collectives, per_device(): partial = lax.all_to_all(partial.reshape(groups, group, docs), 'term', 0, 0)  17.8 us
    all_to_all x1, blocking collectives, per_device(): lax.all_to_all(jnp.broadcast_to(expanded[None], (blocks, chunk, width)),...  14.7 us
    pallas_call x1, Pallas kernels, per_device(): pl.pallas_call(first_round, out_shape=(shape((groups, group // 2, 2 * doc...  2.71 us

profile of v6, /device:TPU:33, one launch (start us, length us, event | category | flops | bytes accessed | tf_op | source)
XLA Modules:
  0.0 87.4 jit_solution(6908902742050430693)
XLA Ops:
  0.6 2.7 %first_round.1 = (s16[16,4,1152]{2,1,0:T(4,128)(2,1)S(1)}, bf16[128,512]{1,0:T(8,128)(2,1)S(1)}, f32[128,1920]{1,0:T(8,128)S(1)}, bf16[512,1920]{1,0:T(8,128)(2,1)S(1)}) custom-call(s32[32,128]{1,0:T(8,128)} %bitcast.7, s32[32,128]{1,0:T(8,128)} %bitcast.8, s32[10,128]{1,0:T(8,128)} %bitcast.9, bf16[512,1920]{1,0:T(8,128)(2,1)} %postings_hbm.1), custom_call_target="tpu_custom_call" | custom-call | tf_op jit(solution)/shard_map/first_round/pallas_call | solution.py:152
  3.4 27.4 %all_to_all.20.received_ref.first_codes_ref = s16[16,4,1152]{2,1,0:T(4,128)(2,1)S(1)} all-to-all(s16[16,4,1152]{2,1,0:T(4,128)(2,1)S(1)} %get-tuple-element.6), channel_id=1, replica_groups=mesh['term'=16,'doc'=32] {'term'}, dimensions={0} | all-to-all | bytes 294912 | tf_op jit(solution)/shard_map/all_to_all | solution.py:174
  30.8 0.5 feedback_round.1
  31.3 21.4 %all_to_all.21.received_ref = bf16[32,4,2048]{2,1,0:T(4,128)(2,1)S(1)} all-to-all(bf16[32,4,2048]{2,1,0:T(4,128)(2,1)S(1)} %feedback_round.1), channel_id=1, replica_groups=mesh['term'=16,'doc'=32] {'doc'}, dimensions={0} | all-to-all | bytes 1048576 | tf_op jit(solution)/shard_map/all_to_all | solution.py:183
  52.7 0.2 expand.1
  52.9 0.1 broadcast_in_dim.2
  53.1 14.7 %all_to_all.22 = bf16[32,4,1920]{2,1,0:T(4,128)(2,1)S(1)} all-to-all(bf16[32,4,1920]{2,1,0:T(4,128)(2,1)S(1)} %broadcast_in_dim.2), channel_id=1, replica_groups=mesh['term'=16,'doc'=32] {'doc'}, dimensions={0} | all-to-all | bytes 983040 | tf_op jit(solution)/shard_map/all_to_all | solution.py:192
  67.8 0.1 reshape.11
  67.9 0.9 %fusion.6 = s16[16,8,512]{2,1,0:T(8,128)(2,1)S(1)} fusion(bf16[128,1920]{1,0:T(8,128)(2,1)S(1)} %reshape.11, bf16[512,1920]{1,0:T(8,128)(2,1)S(1)} %get-tuple-element.8.postings_ref), kind=kOutput, calls=%fused_computation.10 | convolution fusion | flops 252313600 | bytes 2588672 | tf_op jit(solution)/shard_map/dot_general | solution.py:19
  68.8 17.8 %all_to_all.23.final_codes_ref = s16[16,8,512]{2,1,0:T(8,128)(2,1)S(1)} all-to-all(s16[16,8,512]{2,1,0:T(8,128)(2,1)S(1)} %fusion.6), channel_id=1, replica_groups=mesh['term'=16,'doc'=32] {'term'}, dimensions={0} | all-to-all | bytes 262144 | tf_op jit(solution)/shard_map/all_to_all | solution.py:194
  86.6 0.7 totals.1

commit v7 on v6

--- a/solution.py
+++ b/solution.py
@@ -129,7 +129,7 @@
 
 
 def expand(received_ref, query_ref, out_ref):
-    chunk, width = out_ref.shape
+    blocks, chunk, width = out_ref.shape
     total = received_ref[0].astype(f32)
     for d in range(1, received_ref.shape[0]):
         total = total + received_ref[d].astype(f32)
@@ -137,7 +137,19 @@
     doc = lax.axis_index("doc")
     pair = query_ref[pl.ds(pl.multiple_of(lax.shift_right_logical(doc, 1) * 8, 8), 8), :]
     mine = jnp.where((doc & 1) == 0, pair[:chunk], pair[chunk:])
-    out_ref[...] = (mine + expansion_weight * total[:, :width] / weight).astype(bf16)
+    mine = (mine + expansion_weight * total[:, :width] / weight).astype(bf16)
+    for d in range(blocks):
+        out_ref[d] = mine
+
+
+def rescore(gathered_ref, postings_ref, send_ref, rows_ref, *, final_top):
+    chunk = gathered_ref.shape[1]
+    for d in range(gathered_ref.shape[0]):
+        rows_ref[chunk * d : chunk * d + chunk] = gathered_ref[d]
+    codes = encode(dot_nt(rows_ref[...], postings_ref[...]), final_top)
+    group = send_ref.shape[1]
+    for g in range(send_ref.shape[0]):
+        send_ref[g] = codes[group * g : group * g + group]
 
 
 def per_device(postings, query_terms, query_levels, feedback_ids):
@@ -183,15 +195,23 @@
     received = lax.all_to_all(send, "doc", 0, 0)
     expanded = pl.pallas_call(
         expand,
-        out_shape=shape((chunk, width), bf16),
+        out_shape=shape((blocks, chunk, width), bf16),
         in_specs=[VMEM] * 2,
         out_specs=VMEM,
         compiler_params=pltpu.CompilerParams(vmem_limit_bytes=32 << 20),
         name="expand",
     )(received, query)
-    gathered = lax.all_to_all(jnp.broadcast_to(expanded[None], (blocks, chunk, width)), "doc", 0, 0)
-    partial = encode(dot_nt(gathered.reshape(queries, width), postings), final_top)
-    partial = lax.all_to_all(partial.reshape(groups, group, docs), "term", 0, 0)
+    gathered = lax.all_to_all(expanded, "doc", 0, 0)
+    send = pl.pallas_call(
+        functools.partial(rescore, final_top=final_top),
+        out_shape=shape((groups, group, docs), jnp.int16),
+        in_specs=[VMEM] * 2,
+        out_specs=VMEM,
+        scratch_shapes=[pltpu.VMEM((queries, width), bf16)],
+        compiler_params=pltpu.CompilerParams(vmem_limit_bytes=32 << 20),
+        name="rescore",
+    )(gathered, postings)
+    partial = lax.all_to_all(send, "term", 0, 0)
     return pl.pallas_call(
         functools.partial(totals, final_top=final_top),
         out_shape=(shape((group, docs), f32),) * 2,

time: 87.7 us -> 87.5 us (level)
  Pallas kernels: 4.15 us -> 5.07 us
  matrix products: 0.89 us -> 0 us
    pallas_call x1 -> x2, Pallas kernels: 0.18 us -> 1.11 us  [the longest x1 0.89 us: per_device(): pl.pallas_call(functools.partial(rescore, final_top=final_top), out_shape...]
    dot_general x1 -> x0, matrix products: 0.89 us -> none  [dot_nt(): lax.dot_general(a, b, (((1,), (1,)), ((), ())), preferred_element_type=f32)]
where the time goes in v7:
time: 87.5 us; the launch traced here: 87.2 us
  blocking collectives  81.4 us (93%)
  Pallas kernels  5.07 us (6%)
    all_to_all x1, blocking collectives, per_device(): first_codes = lax.all_to_all(send, 'term', 0, 0)  27.4 us
    all_to_all x1, blocking collectives, per_device(): received = lax.all_to_all(send, 'doc', 0, 0)  21.4 us
    all_to_all x1, blocking collectives, per_device(): partial = lax.all_to_all(send, 'term', 0, 0)  17.8 us
    all_to_all x1, blocking collectives, per_device(): gathered = lax.all_to_all(expanded, 'doc', 0, 0)  14.7 us
    pallas_call x1, Pallas kernels, per_device(): pl.pallas_call(first_round, out_shape=(shape((groups, group // 2, 2 * doc...  2.71 us

profile of v7, /device:TPU:33, one launch (start us, length us, event | category | flops | bytes accessed | tf_op | source)
XLA Modules:
  0.0 87.2 jit_solution(9472492028067006991)
XLA Ops:
  0.6 2.7 %first_round.1 = (s16[16,4,1152]{2,1,0:T(4,128)(2,1)S(1)}, bf16[128,512]{1,0:T(8,128)(2,1)S(1)}, f32[128,1920]{1,0:T(8,128)S(1)}, bf16[512,1920]{1,0:T(8,128)(2,1)S(1)}) custom-call(s32[32,128]{1,0:T(8,128)} %bitcast.3, s32[32,128]{1,0:T(8,128)} %bitcast.4, s32[10,128]{1,0:T(8,128)} %bitcast.5, bf16[512,1920]{1,0:T(8,128)(2,1)} %postings_hbm.1), custom_call_target="tpu_custom_call" | custom-call | tf_op jit(solution)/shard_map/first_round/pallas_call | solution.py:164
  3.4 27.4 %all_to_all.20.received_ref.first_codes_ref = s16[16,4,1152]{2,1,0:T(4,128)(2,1)S(1)} all-to-all(s16[16,4,1152]{2,1,0:T(4,128)(2,1)S(1)} %get-tuple-element.6), channel_id=1, replica_groups=mesh['term'=16,'doc'=32] {'term'}, dimensions={0} | all-to-all | bytes 294912 | tf_op jit(solution)/shard_map/all_to_all | solution.py:186
  30.8 0.5 feedback_round.1
  31.3 21.4 %all_to_all.21.received_ref = bf16[32,4,2048]{2,1,0:T(4,128)(2,1)S(1)} all-to-all(bf16[32,4,2048]{2,1,0:T(4,128)(2,1)S(1)} %feedback_round.1), channel_id=1, replica_groups=mesh['term'=16,'doc'=32] {'doc'}, dimensions={0} | all-to-all | bytes 1048576 | tf_op jit(solution)/shard_map/all_to_all | solution.py:195
  52.7 0.2 expand.1
  53.0 14.7 %all_to_all.22.gathered_ref = bf16[32,4,1920]{2,1,0:T(4,128)(2,1)S(1)} all-to-all(bf16[32,4,1920]{2,1,0:T(4,128)(2,1)S(1)} %expand.1), channel_id=1, replica_groups=mesh['term'=16,'doc'=32] {'doc'}, dimensions={0} | all-to-all | bytes 983040 | tf_op jit(solution)/shard_map/all_to_all | solution.py:204
  67.7 0.9 %rescore.1 = s16[16,8,512]{2,1,0:T(8,128)(2,1)S(1)} custom-call(bf16[32,4,1920]{2,1,0:T(4,128)(2,1)S(1)} %all_to_all.22.gathered_ref, bf16[512,1920]{1,0:T(8,128)(2,1)S(1)} %get-tuple-element.8.postings_ref), custom_call_target="tpu_custom_call" | custom-call | tf_op jit(solution)/shard_map/rescore/pallas_call | solution.py:205
  68.6 17.8 %all_to_all.23.final_codes_ref = s16[16,8,512]{2,1,0:T(8,128)(2,1)S(1)} all-to-all(s16[16,8,512]{2,1,0:T(8,128)(2,1)S(1)} %rescore.1), channel_id=1, replica_groups=mesh['term'=16,'doc'=32] {'term'}, dimensions={0} | all-to-all | bytes 262144 | tf_op jit(solution)/shard_map/all_to_all | solution.py:214
  86.4 0.7 totals.1

commit v8 on v7

--- a/solution.py
+++ b/solution.py
@@ -46,6 +46,7 @@
         copy.start()
     copies[0].wait()
     copies[1].wait()
+    copies[2].wait()
     slots, queries = terms_ref.shape
     docs, width = postings_ref.shape
     tiles = width // lanes
@@ -70,7 +71,6 @@
         totals = dot_nt(jnp.concatenate(parts, axis=0).astype(bf16), hot)
         for t in range(tiles):
             query_ref[rows, t * lanes : (t + 1) * lanes] = totals[8 * t : 8 * t + 8] * f32(0.01)
-    copies[2].wait()
     place = (iota((docs, queries), 0) + lax.axis_index("doc") * docs).astype(jnp.int16)
     ids = ids_ref[...].astype(jnp.int16)
     member = ids[0:1, :] == place

time: 87.5 us -> 87.3 us (level)
  no operation moved by 1% of the time
where the time goes in v8:
time: 87.3 us; the launch traced here: 87 us
  blocking collectives  81.4 us (93%)
  Pallas kernels  4.9 us (6%)
    all_to_all x1, blocking collectives, per_device(): first_codes = lax.all_to_all(send, 'term', 0, 0)  27.4 us
    all_to_all x1, blocking collectives, per_device(): received = lax.all_to_all(send, 'doc', 0, 0)  21.4 us
    all_to_all x1, blocking collectives, per_device(): partial = lax.all_to_all(send, 'term', 0, 0)  17.8 us
    all_to_all x1, blocking collectives, per_device(): gathered = lax.all_to_all(expanded, 'doc', 0, 0)  14.7 us
    pallas_call x1, Pallas kernels, per_device(): pl.pallas_call(first_round, out_shape=(shape((groups, group // 2, 2 * doc...  2.54 us

profile of v8, /device:TPU:33, one launch (start us, length us, event | category | flops | bytes accessed | tf_op | source)
XLA Modules:
  0.0 87.0 jit_solution(15240782838938548926)
XLA Ops:
  0.6 2.5 %first_round.1 = (s16[16,4,1152]{2,1,0:T(4,128)(2,1)S(1)}, bf16[128,512]{1,0:T(8,128)(2,1)S(1)}, f32[128,1920]{1,0:T(8,128)S(1)}, bf16[512,1920]{1,0:T(8,128)(2,1)S(1)}) custom-call(s32[32,128]{1,0:T(8,128)} %bitcast.3, s32[32,128]{1,0:T(8,128)} %bitcast.4, s32[10,128]{1,0:T(8,128)} %bitcast.5, bf16[512,1920]{1,0:T(8,128)(2,1)} %postings_hbm.1), custom_call_target="tpu_custom_call" | custom-call | tf_op jit(solution)/shard_map/first_round/pallas_call | solution.py:164
  3.2 27.4 %all_to_all.20.received_ref.first_codes_ref = s16[16,4,1152]{2,1,0:T(4,128)(2,1)S(1)} all-to-all(s16[16,4,1152]{2,1,0:T(4,128)(2,1)S(1)} %get-tuple-element.6), channel_id=1, replica_groups=mesh['term'=16,'doc'=32] {'term'}, dimensions={0} | all-to-all | bytes 294912 | tf_op jit(solution)/shard_map/all_to_all | solution.py:186
  30.6 0.5 feedback_round.1
  31.1 21.4 %all_to_all.21.received_ref = bf16[32,4,2048]{2,1,0:T(4,128)(2,1)S(1)} all-to-all(bf16[32,4,2048]{2,1,0:T(4,128)(2,1)S(1)} %feedback_round.1), channel_id=1, replica_groups=mesh['term'=16,'doc'=32] {'doc'}, dimensions={0} | all-to-all | bytes 1048576 | tf_op jit(solution)/shard_map/all_to_all | solution.py:195
  52.6 0.2 expand.1
  52.8 14.7 %all_to_all.22.gathered_ref = bf16[32,4,1920]{2,1,0:T(4,128)(2,1)S(1)} all-to-all(bf16[32,4,1920]{2,1,0:T(4,128)(2,1)S(1)} %expand.1), channel_id=1, replica_groups=mesh['term'=16,'doc'=32] {'doc'}, dimensions={0} | all-to-all | bytes 983040 | tf_op jit(solution)/shard_map/all_to_all | solution.py:204
  67.5 0.9 %rescore.1 = s16[16,8,512]{2,1,0:T(8,128)(2,1)S(1)} custom-call(bf16[32,4,1920]{2,1,0:T(4,128)(2,1)S(1)} %all_to_all.22.gathered_ref, bf16[512,1920]{1,0:T(8,128)(2,1)S(1)} %get-tuple-element.8.postings_ref), custom_call_target="tpu_custom_call" | custom-call | tf_op jit(solution)/shard_map/rescore/pallas_call | solution.py:205
  68.4 17.8 %all_to_all.23.final_codes_ref = s16[16,8,512]{2,1,0:T(8,128)(2,1)S(1)} all-to-all(s16[16,8,512]{2,1,0:T(8,128)(2,1)S(1)} %rescore.1), channel_id=1, replica_groups=mesh['term'=16,'doc'=32] {'term'}, dimensions={0} | all-to-all | bytes 262144 | tf_op jit(solution)/shard_map/all_to_all | solution.py:214
  86.3 0.7 totals.1

commit v9 on v8

--- a/solution.py
+++ b/solution.py
@@ -58,7 +58,7 @@
     stacked = jnp.concatenate([tile_of, lane_of, levels_ref[...]], axis=1).astype(f32).astype(bf16)
     wide = lax.dot_general(stacked, repeat, (((0,), (0,)), ((), ())), preferred_element_type=f32)
     own = lax.shift_right_logical(iota((8, spread), 1), 5) == iota((8, spread), 0)
-    lane_ids = iota((lanes, spread), 0).astype(f32)
+    lane_ids = iota((lanes, spread), 0).astype(f32).astype(bf16)
     for block in range(queries // 8):
         rows = slice(8 * block, 8 * block + 8)
         tile_now = wide[rows]
@@ -66,7 +66,7 @@
         level_now = wide[2 * queries + 8 * block : 2 * queries + 8 * block + 8]
         lane_row = jnp.sum(jnp.where(own, lane_now, 0.0), axis=0, keepdims=True)
         level_own = jnp.where(own, level_now, 0.0)
-        hot = jnp.where(lane_ids == lane_row, 1.0, 0.0).astype(bf16)
+        hot = jnp.where(lane_ids == lane_row.astype(bf16), jnp.ones((), bf16), jnp.zeros((), bf16))
         parts = [jnp.where(tile_now == float(t), level_own, 0.0) for t in range(tiles)]
         totals = dot_nt(jnp.concatenate(parts, axis=0).astype(bf16), hot)
         for t in range(tiles):

time: 87.3 us -> 87.3 us (level)
  no operation moved by 1% of the time
where the time goes in v9:
time: 87.3 us; the launch traced here: 87 us
  blocking collectives  81.4 us (93%)
  Pallas kernels  4.9 us (6%)
    all_to_all x1, blocking collectives, per_device(): first_codes = lax.all_to_all(send, 'term', 0, 0)  27.4 us
    all_to_all x1, blocking collectives, per_device(): received = lax.all_to_all(send, 'doc', 0, 0)  21.4 us
    all_to_all x1, blocking collectives, per_device(): partial = lax.all_to_all(send, 'term', 0, 0)  17.8 us
    all_to_all x1, blocking collectives, per_device(): gathered = lax.all_to_all(expanded, 'doc', 0, 0)  14.7 us
    pallas_call x1, Pallas kernels, per_device(): pl.pallas_call(first_round, out_shape=(shape((groups, group // 2, 2 * doc...  2.54 us

profile of v9, /device:TPU:33, one launch (start us, length us, event | category | flops | bytes accessed | tf_op | source)
XLA Modules:
  0.0 87.0 jit_solution(18442271134572819854)
XLA Ops:
  0.6 2.5 %first_round.1 = (s16[16,4,1152]{2,1,0:T(4,128)(2,1)S(1)}, bf16[128,512]{1,0:T(8,128)(2,1)S(1)}, f32[128,1920]{1,0:T(8,128)S(1)}, bf16[512,1920]{1,0:T(8,128)(2,1)S(1)}) custom-call(s32[32,128]{1,0:T(8,128)} %bitcast.3, s32[32,128]{1,0:T(8,128)} %bitcast.4, s32[10,128]{1,0:T(8,128)} %bitcast.5, bf16[512,1920]{1,0:T(8,128)(2,1)} %postings_hbm.1), custom_call_target="tpu_custom_call" | custom-call | tf_op jit(solution)/shard_map/first_round/pallas_call | solution.py:164
  3.2 27.4 %all_to_all.20.received_ref.first_codes_ref = s16[16,4,1152]{2,1,0:T(4,128)(2,1)S(1)} all-to-all(s16[16,4,1152]{2,1,0:T(4,128)(2,1)S(1)} %get-tuple-element.6), channel_id=1, replica_groups=mesh['term'=16,'doc'=32] {'term'}, dimensions={0} | all-to-all | bytes 294912 | tf_op jit(solution)/shard_map/all_to_all | solution.py:186
  30.6 0.5 feedback_round.1
  31.1 21.4 %all_to_all.21.received_ref = bf16[32,4,2048]{2,1,0:T(4,128)(2,1)S(1)} all-to-all(bf16[32,4,2048]{2,1,0:T(4,128)(2,1)S(1)} %feedback_round.1), channel_id=1, replica_groups=mesh['term'=16,'doc'=32] {'doc'}, dimensions={0} | all-to-all | bytes 1048576 | tf_op jit(solution)/shard_map/all_to_all | solution.py:195
  52.6 0.2 expand.1
  52.8 14.7 %all_to_all.22.gathered_ref = bf16[32,4,1920]{2,1,0:T(4,128)(2,1)S(1)} all-to-all(bf16[32,4,1920]{2,1,0:T(4,128)(2,1)S(1)} %expand.1), channel_id=1, replica_groups=mesh['term'=16,'doc'=32] {'doc'}, dimensions={0} | all-to-all | bytes 983040 | tf_op jit(solution)/shard_map/all_to_all | solution.py:204
  67.5 0.9 %rescore.1 = s16[16,8,512]{2,1,0:T(8,128)(2,1)S(1)} custom-call(bf16[32,4,1920]{2,1,0:T(4,128)(2,1)S(1)} %all_to_all.22.gathered_ref, bf16[512,1920]{1,0:T(8,128)(2,1)S(1)} %get-tuple-element.8.postings_ref), custom_call_target="tpu_custom_call" | custom-call | tf_op jit(solution)/shard_map/rescore/pallas_call | solution.py:205
  68.4 17.8 %all_to_all.23.final_codes_ref = s16[16,8,512]{2,1,0:T(8,128)(2,1)S(1)} all-to-all(s16[16,8,512]{2,1,0:T(8,128)(2,1)S(1)} %rescore.1), channel_id=1, replica_groups=mesh['term'=16,'doc'=32] {'term'}, dimensions={0} | all-to-all | bytes 262144 | tf_op jit(solution)/shard_map/all_to_all | solution.py:214
  86.3 0.7 totals.1
